TPU v7x, 256 devices: a whole 4x4x8 slice. The times are simulated.
256 devices in a mesh: dp: 2 (over core), row: 16 (over x, y), col: 8 (over z).
Axes of the slice: x: 4, y: 4, z: 8, core: 2. Of those that a mesh axis runs over, the one named last changes fastest.
Arguments:
- tokens: bfloat16 [1536, 8192], P('dp', 'row'), may hold values from -6 to 6
- out_grad: bfloat16 [1536, 8192], P('dp', 'row'), may hold values from -6 to 6
- gate_weight: bfloat16 [8192, 14336], P('row', 'col'), may hold values from -0.0625 to 0.0625
- up_weight: bfloat16 [8192, 14336], P('row', 'col'), may hold values from -0.0625 to 0.0625
- down_weight: bfloat16 [14336, 8192], P('col', 'row'), may hold values from -0.046875 to 0.046875
- gate_mask: int32 [64, 112], P('row', 'col'), may hold values from 0 to 1, as said below
- up_mask: int32 [64, 112], P('row', 'col'), may hold values from 0 to 1, as said below
- down_mask: int32 [112, 64], P('col', 'row'), may hold values from 0 to 1, as said below
Outputs:
- output: bfloat16 [1536, 8192], P(('dp', 'col'), 'row')
- token_grad: bfloat16 [1536, 8192], P(('dp', 'col'), 'row')
- gate_grad: bfloat16 [8192, 14336], P('row', 'col')
- up_grad: bfloat16 [8192, 14336], P('row', 'col')
- down_grad: bfloat16 [14336, 8192], P('col', 'row')
Inputs may be any that keep to these rules, and one draw needn't show every extreme that they name: `gate_mask`: one keep flag for each 128 x 128 block of the matrix; the share kept differs from block row to block row. `up_mask`: one keep flag for each 128 x 128 block of the matrix; the share kept differs from block row to block row. `down_mask`: one keep flag for each 128 x 128 block of the matrix; the share kept differs from block column to block column.
All inputs are finite; a program needn't handle non-finite values.
Results may differ from a plain program's by a relative error of at most 0.029.
Values may be sent and summed in bfloat16 or wider, within the bound.
A program may use at most 128 MiB of HBM per device.

v0:
```python
import jax
import jax.numpy as jnp
from jax import lax
from jax.sharding import PartitionSpec as P

BLOCK = 128


def expand(mask_tile):
    return jnp.repeat(jnp.repeat(mask_tile, BLOCK, axis=0), BLOCK, axis=1)


def contract_rows(left_side, right_side):
    return lax.dot_general(
        left_side, right_side, (((0,), (0,)), ((), ())), preferred_element_type=jnp.float32
    )


def contract_cols(left_side, right_side):
    return lax.dot_general(
        left_side, right_side, (((1,), (1,)), ((), ())), preferred_element_type=jnp.float32
    )


def body(tokens, out_grad, gate_weight, up_weight, down_weight, gate_mask, up_mask, down_mask):
    gate_keep = expand(gate_mask)
    up_keep = expand(up_mask)
    down_keep = expand(down_mask)
    gate_eff = gate_weight * gate_keep.astype(jnp.bfloat16)
    up_eff = up_weight * up_keep.astype(jnp.bfloat16)
    down_eff = down_weight * down_keep.astype(jnp.bfloat16)
    gate_part = jnp.dot(tokens, gate_eff, preferred_element_type=jnp.float32)
    up_part = jnp.dot(tokens, up_eff, preferred_element_type=jnp.float32)
    gate_share, up_share = (
        lax.psum_scatter(
            gate_part.astype(jnp.bfloat16), "row", scatter_dimension=0, tiled=True
        ).astype(jnp.float32),
        lax.psum_scatter(
            up_part.astype(jnp.bfloat16), "row", scatter_dimension=0, tiled=True
        ).astype(jnp.float32),
    )
    gate_sig = jax.nn.sigmoid(gate_share)
    silu_gate = gate_share * gate_sig
    hidden_share = (silu_gate * up_share).astype(jnp.bfloat16)
    hidden = lax.all_gather(hidden_share, "row", axis=0, tiled=True)
    output = lax.psum_scatter(
        jnp.dot(hidden, down_eff, preferred_element_type=jnp.float32).astype(jnp.bfloat16),
        "col",
        scatter_dimension=0,
        tiled=True,
    )
    down_local = contract_rows(hidden, out_grad) * down_keep.astype(jnp.float32)
    back_part = contract_cols(out_grad, down_eff)
    back_share = lax.psum_scatter(
        back_part.astype(jnp.bfloat16), "row", scatter_dimension=0, tiled=True
    ).astype(jnp.float32)
    gate_deriv = (back_share * up_share * gate_sig * (1.0 + gate_share * (1.0 - gate_sig))).astype(
        jnp.bfloat16
    )
    up_deriv = (back_share * silu_gate).astype(jnp.bfloat16)
    gate_full, up_full = (
        lax.all_gather(gate_deriv, "row", axis=0, tiled=True),
        lax.all_gather(up_deriv, "row", axis=0, tiled=True),
    )
    token_grad = lax.psum_scatter(
        (contract_cols(gate_full, gate_eff) + contract_cols(up_full, up_eff)).astype(jnp.bfloat16),
        "col",
        scatter_dimension=0,
        tiled=True,
    )
    gate_local = contract_rows(tokens, gate_full) * gate_keep.astype(jnp.float32)
    up_local = contract_rows(tokens, up_full) * up_keep.astype(jnp.float32)
    gate_total, up_total, down_total = (
        lax.psum(gate_local.astype(jnp.bfloat16), "dp").astype(jnp.float32),
        lax.psum(up_local.astype(jnp.bfloat16), "dp").astype(jnp.float32),
        lax.psum(down_local.astype(jnp.bfloat16), "dp").astype(jnp.float32),
    )
    return (
        output,
        token_grad,
        gate_total.astype(jnp.bfloat16),
        up_total.astype(jnp.bfloat16),
        down_total.astype(jnp.bfloat16),
    )


def solution(mesh):
    placed = (
        P("dp", "row"),
        P("dp", "row"),
        P("row", "col"),
        P("row", "col"),
        P("col", "row"),
        P("row", "col"),
        P("row", "col"),
        P("col", "row"),
    )
    return jax.shard_map(
        body,
        mesh=mesh,
        in_specs=placed,
        out_specs=(
            P(("dp", "col"), "row"),
            P(("dp", "col"), "row"),
            P("row", "col"),
            P("row", "col"),
            P("col", "row"),
        ),
        check_vma=False,
    )
```

profile of v0, /device:TPU:2, one launch (start us, length us, event | category | flops | bytes accessed | tf_op | source)
XLA Modules:
  0.0 568.2 jit_solution(9316289985637627538)
XLA Ops:
  8.2 5.1 broadcast_in_dim.35
  13.3 1.2 copy-done.8
  14.5 1.6 fusion.5
  16.2 2.9 copy.59
  19.1 2.8 copy.43
  22.3 1.2 copy-done.4
  23.6 1.6 fusion.3
  25.2 2.9 copy.55
  28.2 2.8 copy.46
  31.4 1.2 copy-done.5
  32.6 1.6 fusion.4
  34.2 2.9 copy.57
  37.2 66.0 %reduce-scatter.20.cloned.1.call-done = bf16[48,1792]{1,0:T(8,128)(2,1)} async-done(((bf16[768,1792]{1,0:T(8,128)(2,1)}), bf16[48,1792]{1,0:T(8,128)(2,1)}) %reduce-scatter.20.cloned.1.call-update) | async-done | bytes 172048 | tf_op jit(solution)/shard_map/reduce_scatter | solution.py:54
  103.2 84.2 %reduce-scatter.16.cloned.1.call-done = bf16[48,1792]{1,0:T(8,128)(2,1)} async-done(((bf16[768,1792]{1,0:T(8,128)(2,1)}), bf16[48,1792]{1,0:T(8,128)(2,1)}) %reduce-scatter.16.cloned.1.call-update) | async-done | bytes 172048 | tf_op jit(solution)/shard_map/reduce_scatter | solution.py:35
  187.5 84.3 %reduce-scatter.18.cloned.1.call-done = bf16[48,1792]{1,0:T(8,128)(2,1)} async-done(((bf16[768,1792]{1,0:T(8,128)(2,1)}), bf16[48,1792]{1,0:T(8,128)(2,1)}) %reduce-scatter.18.cloned.1.call-update) | async-done | bytes 172048 | tf_op jit(solution)/shard_map/reduce_scatter | solution.py:38
  271.7 2.1 fusion.10
  275.7 48.8 %all-gather.6.cloned.1.call-done = bf16[768,1792]{1,0:T(8,128)(2,1)} async-done(((bf16[48,1792]{1,0:T(8,128)(2,1)}), bf16[768,1792]{1,0:T(8,128)(2,1)}) %all-gather.6.cloned.1.call-update) | async-done | bytes 2752528 | tf_op jit(solution)/shard_map/all_gather | solution.py:62
  324.5 4.7 fusion.2
  329.2 48.4 %all-gather.8.cloned.1.call-done = bf16[768,1792]{1,0:T(8,128)(2,1)} async-done(((bf16[48,1792]{1,0:T(8,128)(2,1)}), bf16[768,1792]{1,0:T(8,128)(2,1)}) %all-gather.8.cloned.1.call-update) | async-done | bytes 2752528 | tf_op jit(solution)/shard_map/all_gather | solution.py:63
  377.6 4.7 fusion.1
  382.3 48.4 %all-gather.4.cloned.1.call-done = bf16[768,1792]{1,0:T(8,128)(2,1)} async-done(((bf16[48,1792]{1,0:T(8,128)(2,1)}), bf16[768,1792]{1,0:T(8,128)(2,1)}) %all-gather.4.cloned.1.call-update) | async-done | bytes 2752528 | tf_op jit(solution)/shard_map/all_gather | solution.py:45
  430.8 2.2 broadcast_in_dim.41
  433.0 2.9 fusion
  436.0 5.5 convolution_convert_fusion.3
  441.6 3.2 fusion.18
  444.8 2.5 add_convert_fusion
  447.3 29.8 %all-reduce.3.cloned.1.call-done = (bf16[512,1792]{0,1:T(8,128)(2,1)}, bf16[512,1792]{0,1:T(8,128)(2,1)}, bf16[1792,512]{1,0:T(8,128)(2,1)}) async-done(((bf16[512,1792]{0,1:T(8,128)(2,1)}, bf16[512,1792]{0,1:T(8,128)(2,1)}, bf16[1792,512]{1,0:T(8,128)(2,1)}), (bf16[512,1792]{0,1:T(8,128)(2,1)}, bf16[512,1792]{0,1:T(8,128)(2,1)}, bf16[1792,512]{1,0:T(8,128)(2,1)})) %all-reduce.3.cloned.1.call-update) | async-done | bytes 5505040 | tf_op jit(solution)/shard_map/psum | solution.py:74
  477.1 3.8 copy.53
  480.9 3.9 copy.54
  484.8 35.0 %reduce-scatter.12.cloned.1.call-done = bf16[96,512]{1,0:T(8,128)(2,1)} async-done(((bf16[768,512]{1,0:T(8,128)(2,1)}), bf16[96,512]{1,0:T(8,128)(2,1)}) %reduce-scatter.12.cloned.1.call-update) | async-done | bytes 98320 | tf_op jit(solution)/shard_map/reduce_scatter | solution.py:46
  519.9 40.1 %reduce-scatter.14.cloned.1.call-done = bf16[96,512]{1,0:T(8,128)(2,1)} async-done(((bf16[768,512]{1,0:T(8,128)(2,1)}), bf16[96,512]{1,0:T(8,128)(2,1)}) %reduce-scatter.14.cloned.1.call-update) | async-done | bytes 98320 | tf_op jit(solution)/shard_map/reduce_scatter | solution.py:65
  560.0 1.2 copy.74
  (70 shorter events, 4.4 us)
Async XLA Ops:
  7.2 16.4 %copy-start = (bf16[768,512]{1,0:T(8,128)(2,1)S(1)}, bf16[768,512]{1,0:T(8,128)(2,1)}, u32[]{:S(2)}) copy-start(bf16[768,512]{1,0:T(8,128)(2,1)} %param.8) | copy-start | bytes 2359300
  7.2 96.1 %reduce-scatter.20.cloned.1.call-start = ((), (), s32[]{:S(2)}) async-start(), calls=%async_computation.12 | async-start | bytes 2924544 | tf_op jit(solution)/shard_map/reduce_scatter | solution.py:54
  8.1 6.4 %copy-start.12 = (bf16[1792,512]{1,0:T(8,128)(2,1)S(1)}, bf16[1792,512]{1,0:T(8,128)(2,1)}, u32[]{:S(2)}) copy-start(bf16[1792,512]{1,0:T(8,128)(2,1)} %param.12) | copy-start | bytes 5505028
  8.1 6.4 %copy-start.13 = (bf16[768,512]{1,0:T(8,128)(2,1)S(1)}, bf16[768,512]{1,0:T(8,128)(2,1)}, u32[]{:S(2)}) copy-start(bf16[768,512]{1,0:T(8,128)(2,1)} %param.9) | copy-start | bytes 2359300
  13.3 1.2 copy-start.8
  19.1 2.9 copy-start.9
  19.1 168.4 %reduce-scatter.16.cloned.1.call-start = ((), (), s32[]{:S(2)}) async-start(), calls=%async_computation.10 | async-start | bytes 2924544 | tf_op jit(solution)/shard_map/reduce_scatter | solution.py:35
  22.3 1.2 copy-start.4
  28.1 2.9 copy-start.10
  28.1 243.6 %reduce-scatter.18.cloned.1.call-start = ((), (), s32[]{:S(2)}) async-start(), calls=%async_computation.11 | async-start | bytes 2924544 | tf_op jit(solution)/shard_map/reduce_scatter | solution.py:38
  31.4 1.2 copy-start.5
  37.2 287.3 %all-gather.6.cloned.1.call-start = ((), (), s32[]{:S(2)}) async-start(), calls=%async_computation.7 | async-start | bytes 2924544 | tf_op jit(solution)/shard_map/all_gather | solution.py:62
  273.8 103.8 %all-gather.8.cloned.1.call-start = ((), (), s32[]{:S(2)}) async-start(), calls=%async_computation.8 | async-start | bytes 2924544 | tf_op jit(solution)/shard_map/all_gather | solution.py:63
  274.4 156.3 %all-gather.4.cloned.1.call-start = ((), (), s32[]{:S(2)}) async-start(), calls=%async_computation.5 | async-start | bytes 2924544 | tf_op jit(solution)/shard_map/all_gather | solution.py:45
  275.0 202.1 %all-reduce.3.cloned.1.call-start = ((), (), s32[]{:S(2)}) async-start(), calls=%async_computation.13 | async-start | bytes 11010048 | tf_op jit(solution)/shard_map/psum | solution.py:74
  430.7 2.2 copy-start.11
  430.8 2.2 copy-start.14
  435.9 5.7 copy-start.2
  435.9 83.9 %reduce-scatter.12.cloned.1.call-start = ((), (), s32[]{:S(2)}) async-start(), calls=%async_computation.6 | async-start | bytes 884736 | tf_op jit(solution)/shard_map/reduce_scatter | solution.py:46
  441.5 118.5 %reduce-scatter.14.cloned.1.call-start = ((), (), s32[]{:S(2)}) async-start(), calls=%async_computation.9 | async-start | bytes 884736 | tf_op jit(solution)/shard_map/reduce_scatter | solution.py:65
  441.6 3.3 copy-start.3
  441.6 3.3 copy-start.6
  480.9 79.1 %copy-start.7 = (bf16[1792,512]{1,0:T(8,128)(2,1)S(1)}, bf16[1792,512]{1,0:T(8,128)(2,1)}, u32[]{:S(2)}) copy-start(bf16[1792,512]{1,0:T(8,128)(2,1)} %get-tuple-element.41) | copy-start | bytes 5505028
  560.0 1.7 copy-start.1
Sparse Core Ops, SparseCore 0:
  19.2 84.0 reduce-scatter.19
  106.8 80.5 reduce-scatter.15
  191.1 80.5 reduce-scatter.17
  274.1 50.4 all-gather.5
  326.9 50.6 all-gather.7
  379.9 50.6 all-gather.3
  436.0 41.0 all-reduce.2
  480.2 39.6 reduce-scatter.11
  523.0 36.9 reduce-scatter.13
where the time goes:
time: 569 us; the launch traced here: 568 us
  waiting for transfers between devices  486 us (85%)
  local copies, waits for them, and re-layouts  35.8 us (6%)
  matrix products  28.4 us (5%)
  between operations  14.2 us (2%)
    reduce_scatter x1, waiting for transfers between devices, body(): lax.psum_scatter(up_part.astype(jnp.bfloat16), 'row', scatter_dimension=0...  84.3 us
    reduce_scatter x1, waiting for transfers between devices, body(): lax.psum_scatter(gate_part.astype(jnp.bfloat16), 'row', scatter_dimension...  84.2 us
    reduce_scatter x1, waiting for transfers between devices, body(): lax.psum_scatter(back_part.astype(jnp.bfloat16), 'row', scatter_dimension...  66 us
    all_gather x1, waiting for transfers between devices, body(): lax.all_gather(gate_deriv, 'row', axis=0, tiled=True)  48.8 us
    all_gather x1, waiting for transfers between devices, body(): hidden = lax.all_gather(hidden_share, 'row', axis=0, tiled=True)  48.4 us
    all_gather x1, waiting for transfers between devices, body(): lax.all_gather(up_deriv, 'row', axis=0, tiled=True)  48.4 us
    reduce_scatter x1, waiting for transfers between devices, body(): lax.psum_scatter((contract_cols(gate_full, gate_eff) + contract_cols(up_f...  40.1 us
    reduce_scatter x1, waiting for transfers between devices, body(): lax.psum_scatter(jnp.dot(hidden, down_eff, preferred_element_type=jnp.flo...  35 us
  transfers between devices with their start and end apart: 9, of which 9 were waited for; matrix products, arithmetic and copies ran while one was open for 8% of the time, Pallas kernels for 0%

commit v1 on v0

--- a/solution.py
+++ b/solution.py
@@ -4,6 +4,28 @@
 from jax.sharding import PartitionSpec as P
 
 BLOCK = 128
+
+
+def in_order(blocks, dim):
+    dims = list(blocks.shape[1:])
+    dims[dim] *= blocks.shape[0]
+    return jnp.moveaxis(blocks, 0, dim).reshape(dims)
+
+
+def ring_gather(x, axis, dim):
+    length = lax.axis_size(axis)
+    pairs = [(i, (i + 1) % length) for i in range(length)]
+    back = [(b, a) for a, b in pairs]
+    lower, upper = ([], [])
+    for step in range(length - 1):
+        if step % 2 == 0:
+            lower.append(lax.ppermute(lower[-1] if lower else x, axis, pairs))
+        else:
+            upper.append(lax.ppermute(upper[-1] if upper else x, axis, back))
+    blocks = jnp.stack([*lower[::-1], x, *upper])
+    shift = lax.axis_index(axis) - len(lower)
+    blocks = blocks[(jnp.arange(length) - shift) % length]
+    return in_order(blocks, dim)
 
 
 def expand(mask_tile):
@@ -59,7 +81,7 @@
     )
     up_deriv = (back_share * silu_gate).astype(jnp.bfloat16)
     gate_full, up_full = (
-        lax.all_gather(gate_deriv, "row", axis=0, tiled=True),
+        ring_gather(gate_deriv, "row", 0),
         lax.all_gather(up_deriv, "row", axis=0, tiled=True),
     )
     token_grad = lax.psum_scatter(

time: 569 us -> 532 us (0.935)
  waiting for transfers between devices: 486 us -> 402 us
  starting transfers between devices: 0.55 us -> 32.6 us
  local copies, waits for them, and re-layouts: 35.8 us -> 50.7 us
    all_gather x1 -> x0, waiting for transfers between devices: 48.8 us -> none  [body(): lax.all_gather(gate_deriv, 'row', axis=0, tiled=True)]
    all_gather x1, waiting for transfers between devices: 48.4 us -> 0.01 us  [body(): lax.all_gather(up_deriv, 'row', axis=0, tiled=True)]
    ppermute x0 -> x15, waiting for transfers between devices: none -> 34.6 us  [the longest x8 20.7 us: ring_gather(): lower.append(lax.ppermute(lower[-1] if lower else x, axis, pairs))]
    ppermute x0 -> x15, starting transfers between devices: none -> 32.1 us  [the longest x7 31.7 us: ring_gather(): upper.append(lax.ppermute(upper[-1] if upper else x, axis, back))]
    reduce_scatter x1, waiting for transfers between devices: 84.3 us -> 61.6 us  [body(): lax.psum_scatter(up_part.astype(jnp.bfloat16), 'row', scatter_dimension=0...]
    reduce_scatter x1, waiting for transfers between devices: 66 us -> 84.4 us  [body(): lax.psum_scatter(back_part.astype(jnp.bfloat16), 'row', scatter_dimension...]
    all_gather x1, waiting for transfers between devices: 48.4 us -> 32.9 us  [body(): hidden = lax.all_gather(hidden_share, 'row', axis=0, tiled=True)]
    unnamed x50 -> x59, local copies, waits for them, and re-layouts: 27.8 us -> 39.5 us
  transfers between devices with their start and end apart: 9 -> 23, of which waited for: 9 -> 21; matrix products, arithmetic and copies ran while one was open for 8% -> 12% of each run, Pallas kernels for 0% -> 0%
where the time goes in v1:
time: 532 us
  waiting for transfers between devices  402 us (76%)
  local copies, waits for them, and re-layouts  50.7 us (10%)
  starting transfers between devices  32.6 us (6%)
  matrix products  29.6 us (6%)
  between operations  14.4 us (3%)
    reduce_scatter x1, waiting for transfers between devices, body(): lax.psum_scatter(back_part.astype(jnp.bfloat16), 'row', scatter_dimension...  84.4 us
    reduce_scatter x1, waiting for transfers between devices, body(): lax.psum_scatter(gate_part.astype(jnp.bfloat16), 'row', scatter_dimension...  84.3 us
    reduce_scatter x1, waiting for transfers between devices, body(): lax.psum_scatter(up_part.astype(jnp.bfloat16), 'row', scatter_dimension=0...  61.6 us
    reduce_scatter x1, waiting for transfers between devices, body(): lax.psum_scatter((contract_cols(gate_full, gate_eff) + contract_cols(up_f...  40.1 us
    unnamed x59, local copies, waits for them, and re-layouts  39.5 us
    reduce_scatter x1, waiting for transfers between devices, body(): lax.psum_scatter(jnp.dot(hidden, down_eff, preferred_element_type=jnp.flo...  35 us
    all_gather x1, waiting for transfers between devices, body(): hidden = lax.all_gather(hidden_share, 'row', axis=0, tiled=True)  32.9 us
    ppermute x7, starting transfers between devices, ring_gather(): upper.append(lax.ppermute(upper[-1] if upper else x, axis, back))  31.7 us
  transfers between devices with their start and end apart: 23, of which 21 were waited for; matrix products, arithmetic and copies ran while one was open for 12% of the time, Pallas kernels for 0%

profile of v1, /device:TPU:2, one launch (start us, length us, event | category | flops | bytes accessed | tf_op | source)
XLA Modules:
  0.0 531.7 jit_solution(1066148027916991696)
XLA Ops:
  7.2 2.9 copy.62
  13.4 2.8 copy.73
  17.1 5.1 broadcast_in_dim.36
  23.4 3.3 fusion.5
  26.8 2.9 copy.75
  29.8 2.8 copy.59
  35.8 2.9 copy.71
  38.8 61.6 %reduce-scatter.18.cloned.1.call-done = bf16[48,1792]{1,0:T(8,128)(2,1)} async-done(((bf16[768,1792]{1,0:T(8,128)(2,1)}), bf16[48,1792]{1,0:T(8,128)(2,1)}) %reduce-scatter.18.cloned.1.call-update) | async-done | bytes 172048 | tf_op jit(solution)/shard_map/reduce_scatter | solution.py:60
  100.5 84.4 %reduce-scatter.20.cloned.1.call-done = bf16[48,1792]{1,0:T(8,128)(2,1)} async-done(((bf16[768,1792]{1,0:T(8,128)(2,1)}), bf16[48,1792]{1,0:T(8,128)(2,1)}) %reduce-scatter.20.cloned.1.call-update) | async-done | bytes 172048 | tf_op jit(solution)/shard_map/reduce_scatter | solution.py:76
  184.9 84.3 %reduce-scatter.16.cloned.1.call-done = bf16[48,1792]{1,0:T(8,128)(2,1)} async-done(((bf16[768,1792]{1,0:T(8,128)(2,1)}), bf16[48,1792]{1,0:T(8,128)(2,1)}) %reduce-scatter.16.cloned.1.call-update) | async-done | bytes 172048 | tf_op jit(solution)/shard_map/reduce_scatter | solution.py:57
  271.6 7.3 %collective-permute-done = bf16[48,1792]{1,0:T(8,128)(2,1)S(1)} collective-permute-done((bf16[48,1792]{1,0:T(8,128)(2,1)S(1)}, bf16[48,1792]{1,0:T(8,128)(2,1)S(1)}, u32[]{:S(2)}, u32[]{:S(2)}) %collective-permute-start) | collective-permute-done | bytes 172064 | tf_op jit(solution)/shard_map/ppermute | solution.py:22
  278.9 4.1 collective-permute-start.8
  283.0 3.4 collective-permute-done.1
  288.0 4.6 collective-permute-start.9
  297.5 4.6 collective-permute-start.10
  306.0 4.6 collective-permute-start.11
  310.6 3.4 collective-permute-done.4
  314.8 3.6 collective-permute-done.11
  318.4 4.6 collective-permute-start.12
  327.6 4.6 collective-permute-start.13
  335.1 4.6 collective-permute-start.14
  353.2 3.6 fusion.2
  356.9 4.6 fusion.1
  361.5 32.9 %all-gather.3.cloned.1.call-done = bf16[768,1792]{1,0:T(8,128)(2,1)} async-done(((bf16[48,1792]{1,0:T(8,128)(2,1)}), bf16[768,1792]{1,0:T(8,128)(2,1)}) %all-gather.3.cloned.1.call-update) | async-done | bytes 2752528 | tf_op jit(solution)/shard_map/all_gather | solution.py:67
  396.7 2.9 fusion
  399.9 5.4 %convolution_convert_fusion.3 = bf16[768,512]{1,0:T(8,128)(2,1)} fusion(bf16[768,1792]{1,0:T(8,128)(2,1)} %all-gather.3.cloned.1.call-done, bf16[1792,512]{1,0:T(8,128)(2,1)} %param.12, bf16[224,8,4,128]{3,2,1,0:T(4,128)(2,1)} %bitcast.117), kind=kOutput, calls=%fused_computation.17 | convolution fusion | flops 1410596864 | bytes 7208960 | tf_op jit(solution)/shard_map/dot_general | solution.py:69
  405.3 4.0 fusion.20
  411.8 28.9 %all-reduce.3.cloned.1.call-done = (bf16[512,1792]{0,1:T(8,128)(2,1)}, bf16[512,1792]{0,1:T(8,128)(2,1)}, bf16[1792,512]{1,0:T(8,128)(2,1)}) async-done(((bf16[512,1792]{0,1:T(8,128)(2,1)}, bf16[512,1792]{0,1:T(8,128)(2,1)}, bf16[1792,512]{1,0:T(8,128)(2,1)}), (bf16[512,1792]{0,1:T(8,128)(2,1)}, bf16[512,1792]{0,1:T(8,128)(2,1)}, bf16[1792,512]{1,0:T(8,128)(2,1)})) %all-reduce.3.cloned.1.call-update) | async-done | bytes 5505040 | tf_op jit(solution)/shard_map/psum | solution.py:96
  440.8 3.8 copy.69
  444.6 3.9 copy.70
  448.5 35.0 %reduce-scatter.12.cloned.1.call-done = bf16[96,512]{1,0:T(8,128)(2,1)} async-done(((bf16[768,512]{1,0:T(8,128)(2,1)}), bf16[96,512]{1,0:T(8,128)(2,1)}) %reduce-scatter.12.cloned.1.call-update) | async-done | bytes 98320 | tf_op jit(solution)/shard_map/reduce_scatter | solution.py:68
  483.5 40.1 %reduce-scatter.14.cloned.1.call-done = bf16[96,512]{1,0:T(8,128)(2,1)} async-done(((bf16[768,512]{1,0:T(8,128)(2,1)}), bf16[96,512]{1,0:T(8,128)(2,1)}) %reduce-scatter.14.cloned.1.call-update) | async-done | bytes 98320 | tf_op jit(solution)/shard_map/reduce_scatter | solution.py:87
  (110 shorter events, 49.6 us)
Async XLA Ops:
  7.2 4.6 copy-start
  7.2 2.9 copy-start.7
  7.2 93.3 %reduce-scatter.18.cloned.1.call-start = ((), (), s32[]{:S(2)}) async-start(), calls=%async_computation.10 | async-start | bytes 2924544 | tf_op jit(solution)/shard_map/reduce_scatter | solution.py:60
  16.2 168.6 %reduce-scatter.20.cloned.1.call-start = ((), (), s32[]{:S(2)}) async-start(), calls=%async_computation.11 | async-start | bytes 2924544 | tf_op jit(solution)/shard_map/reduce_scatter | solution.py:76
  22.2 1.2 copy-start.6
  29.7 2.9 copy-start.9
  29.7 239.4 %reduce-scatter.16.cloned.1.call-start = ((), (), s32[]{:S(2)}) async-start(), calls=%async_computation.9 | async-start | bytes 2924544 | tf_op jit(solution)/shard_map/reduce_scatter | solution.py:57
  38.8 318.1 %all-gather.5.cloned.1.call-start = ((), (), s32[]{:S(2)}) async-start(), calls=%async_computation.7 | async-start | bytes 2924544 | tf_op jit(solution)/shard_map/all_gather | solution.py:85
  271.2 123.1 %all-gather.3.cloned.1.call-start = ((), (), s32[]{:S(2)}) async-start(), calls=%async_computation.5 | async-start | bytes 2924544 | tf_op jit(solution)/shard_map/all_gather | solution.py:67
  271.3 7.6 %collective-permute-start = (bf16[48,1792]{1,0:T(8,128)(2,1)S(1)}, bf16[48,1792]{1,0:T(8,128)(2,1)S(1)}, u32[]{:S(2)}, u32[]{:S(2)}) collective-permute-start(bf16[48,1792]{1,0:T(8,128)(2,1)S(1)} %get-tuple-element.28), channel_id=1, source_target_pairs={{0,8},{8,16},{16,24},{24,32},{32,40},{40,48},{48,56},{56,64},{64,7... | collective-permute-start | bytes 516104 | tf_op jit(solution)/shard_map/ppermute | solution.py:22
  278.9 7.5 %collective-permute-start.1 = (bf16[48,1792]{1,0:T(8,128)(2,1)S(1)}, bf16[48,1792]{1,0:T(8,128)(2,1)S(1)}, u32[]{:S(2)}, u32[]{:S(2)}) collective-permute-start(bf16[48,1792]{1,0:T(8,128)(2,1)S(1)} %collective-permute-done), channel_id=1, source_target_pairs={{0,8},{8,16},{16,24},{24,32},{32,40},{40,48},{48,56},{56,64},{64,7... | collective-permute-start | bytes 516104 | tf_op jit(solution)/shard_map/ppermute | solution.py:22
  278.9 9.1 %collective-permute-start.8 = (bf16[48,1792]{1,0:T(8,128)(2,1)S(1)}, bf16[48,1792]{1,0:T(8,128)(2,1)S(1)}, u32[]{:S(2)}, u32[]{:S(2)}) collective-permute-start(bf16[48,1792]{1,0:T(8,128)(2,1)S(1)} %get-tuple-element.28), channel_id=1, source_target_pairs={{8,0},{16,8},{24,16},{32,24},{40,32},{48,40},{56,48},{64,56},{72,6... | collective-permute-start | bytes 516104 | tf_op jit(solution)/shard_map/ppermute | solution.py:24
  286.4 9.0 %collective-permute-start.2 = (bf16[48,1792]{1,0:T(8,128)(2,1)S(1)}, bf16[48,1792]{1,0:T(8,128)(2,1)S(1)}, u32[]{:S(2)}, u32[]{:S(2)}) collective-permute-start(bf16[48,1792]{1,0:T(8,128)(2,1)S(1)} %collective-permute-done.1), channel_id=1, source_target_pairs={{0,8},{8,16},{16,24},{24,32},{32,40},{40,48},{48,56},{56,64},{64,7... | collective-permute-start | bytes 516104 | tf_op jit(solution)/shard_map/ppermute | solution.py:22
  288.0 9.5 %collective-permute-start.9 = (bf16[48,1792]{1,0:T(8,128)(2,1)S(1)}, bf16[48,1792]{1,0:T(8,128)(2,1)S(1)}, u32[]{:S(2)}, u32[]{:S(2)}) collective-permute-start(bf16[48,1792]{1,0:T(8,128)(2,1)S(1)} %collective-permute-done.8), channel_id=1, source_target_pairs={{8,0},{16,8},{24,16},{32,24},{40,32},{48,40},{56,48},{64,56},{72,6... | collective-permute-start | bytes 516104 | tf_op jit(solution)/shard_map/ppermute | solution.py:24
  295.4 8.6 %collective-permute-start.3 = (bf16[48,1792]{1,0:T(8,128)(2,1)S(1)}, bf16[48,1792]{1,0:T(8,128)(2,1)S(1)}, u32[]{:S(2)}, u32[]{:S(2)}) collective-permute-start(bf16[48,1792]{1,0:T(8,128)(2,1)S(1)} %collective-permute-done.2), channel_id=1, source_target_pairs={{0,8},{8,16},{16,24},{24,32},{32,40},{40,48},{48,56},{56,64},{64,7... | collective-permute-start | bytes 516104 | tf_op jit(solution)/shard_map/ppermute | solution.py:22
  297.5 8.5 %collective-permute-start.10 = (bf16[48,1792]{1,0:T(8,128)(2,1)S(1)}, bf16[48,1792]{1,0:T(8,128)(2,1)S(1)}, u32[]{:S(2)}, u32[]{:S(2)}) collective-permute-start(bf16[48,1792]{1,0:T(8,128)(2,1)S(1)} %collective-permute-done.9), channel_id=1, source_target_pairs={{8,0},{16,8},{24,16},{32,24},{40,32},{48,40},{56,48},{64,56},{72,6... | collective-permute-start | bytes 516104 | tf_op jit(solution)/shard_map/ppermute | solution.py:24
  304.0 10.0 %collective-permute-start.4 = (bf16[48,1792]{1,0:T(8,128)(2,1)S(1)}, bf16[48,1792]{1,0:T(8,128)(2,1)S(1)}, u32[]{:S(2)}, u32[]{:S(2)}) collective-permute-start(bf16[48,1792]{1,0:T(8,128)(2,1)S(1)} %collective-permute-done.3), channel_id=1, source_target_pairs={{0,8},{8,16},{16,24},{24,32},{32,40},{40,48},{48,56},{56,64},{64,7... | collective-permute-start | bytes 516104 | tf_op jit(solution)/shard_map/ppermute | solution.py:22
  306.0 12.4 %collective-permute-start.11 = (bf16[48,1792]{1,0:T(8,128)(2,1)S(1)}, bf16[48,1792]{1,0:T(8,128)(2,1)S(1)}, u32[]{:S(2)}, u32[]{:S(2)}) collective-permute-start(bf16[48,1792]{1,0:T(8,128)(2,1)S(1)} %collective-permute-done.10), channel_id=1, source_target_pairs={{8,0},{16,8},{24,16},{32,24},{40,32},{48,40},{56,48},{64,56},{72,6... | collective-permute-start | bytes 516104 | tf_op jit(solution)/shard_map/ppermute | solution.py:24
  313.9 10.8 %collective-permute-start.5 = (bf16[48,1792]{1,0:T(8,128)(2,1)S(1)}, bf16[48,1792]{1,0:T(8,128)(2,1)S(1)}, u32[]{:S(2)}, u32[]{:S(2)}) collective-permute-start(bf16[48,1792]{1,0:T(8,128)(2,1)S(1)} %collective-permute-done.4), channel_id=1, source_target_pairs={{0,8},{8,16},{16,24},{24,32},{32,40},{40,48},{48,56},{56,64},{64,7... | collective-permute-start | bytes 516104 | tf_op jit(solution)/shard_map/ppermute | solution.py:22
  318.4 9.2 %collective-permute-start.12 = (bf16[48,1792]{1,0:T(8,128)(2,1)S(1)}, bf16[48,1792]{1,0:T(8,128)(2,1)S(1)}, u32[]{:S(2)}, u32[]{:S(2)}) collective-permute-start(bf16[48,1792]{1,0:T(8,128)(2,1)S(1)} %collective-permute-done.11), channel_id=1, source_target_pairs={{8,0},{16,8},{24,16},{32,24},{40,32},{48,40},{56,48},{64,56},{72,6... | collective-permute-start | bytes 516104 | tf_op jit(solution)/shard_map/ppermute | solution.py:24
  324.7 7.6 %collective-permute-start.6 = (bf16[48,1792]{1,0:T(8,128)(2,1)S(1)}, bf16[48,1792]{1,0:T(8,128)(2,1)S(1)}, u32[]{:S(2)}, u32[]{:S(2)}) collective-permute-start(bf16[48,1792]{1,0:T(8,128)(2,1)S(1)} %collective-permute-done.5), channel_id=1, source_target_pairs={{0,8},{8,16},{16,24},{24,32},{32,40},{40,48},{48,56},{56,64},{64,7... | collective-permute-start | bytes 516104 | tf_op jit(solution)/shard_map/ppermute | solution.py:22
  327.6 7.5 %collective-permute-start.13 = (bf16[48,1792]{1,0:T(8,128)(2,1)S(1)}, bf16[48,1792]{1,0:T(8,128)(2,1)S(1)}, u32[]{:S(2)}, u32[]{:S(2)}) collective-permute-start(bf16[48,1792]{1,0:T(8,128)(2,1)S(1)} %collective-permute-done.12), channel_id=1, source_target_pairs={{8,0},{16,8},{24,16},{32,24},{40,32},{48,40},{56,48},{64,56},{72,6... | collective-permute-start | bytes 516104 | tf_op jit(solution)/shard_map/ppermute | solution.py:24
  332.3 7.5 %collective-permute-start.7 = (bf16[48,1792]{1,0:T(8,128)(2,1)S(1)}, bf16[48,1792]{1,0:T(8,128)(2,1)S(1)}, u32[]{:S(2)}, u32[]{:S(2)}) collective-permute-start(bf16[48,1792]{1,0:T(8,128)(2,1)S(1)} %collective-permute-done.6), channel_id=1, source_target_pairs={{0,8},{8,16},{16,24},{24,32},{32,40},{40,48},{48,56},{56,64},{64,7... | collective-permute-start | bytes 516104 | tf_op jit(solution)/shard_map/ppermute | solution.py:22
  332.4 108.4 %all-reduce.3.cloned.1.call-start = ((), (), s32[]{:S(2)}) async-start(), calls=%async_computation.12 | async-start | bytes 11010048 | tf_op jit(solution)/shard_map/psum | solution.py:96
  335.1 15.0 %collective-permute-start.14 = (bf16[48,1792]{1,0:T(8,128)(2,1)S(1)}, bf16[48,1792]{1,0:T(8,128)(2,1)S(1)}, u32[]{:S(2)}, u32[]{:S(2)}) collective-permute-start(bf16[48,1792]{1,0:T(8,128)(2,1)S(1)} %collective-permute-done.13), channel_id=1, source_target_pairs={{8,0},{16,8},{24,16},{32,24},{40,32},{48,40},{56,48},{64,56},{72,6... | collective-permute-start | bytes 516104 | tf_op jit(solution)/shard_map/ppermute | solution.py:24
  361.5 35.1 %copy-start.11 = (bf16[768,512]{1,0:T(8,128)(2,1)S(1)}, bf16[768,512]{1,0:T(8,128)(2,1)}, u32[]{:S(2)}) copy-start(bf16[768,512]{1,0:T(8,128)(2,1)} %param.9) | copy-start | bytes 2359300
  394.4 2.3 copy-start.10
  399.6 83.9 %reduce-scatter.12.cloned.1.call-start = ((), (), s32[]{:S(2)}) async-start(), calls=%async_computation.6 | async-start | bytes 884736 | tf_op jit(solution)/shard_map/reduce_scatter | solution.py:68
  405.2 118.4 %reduce-scatter.14.cloned.1.call-start = ((), (), s32[]{:S(2)}) async-start(), calls=%async_computation.8 | async-start | bytes 884736 | tf_op jit(solution)/shard_map/reduce_scatter | solution.py:87
  405.3 4.1 copy-start.4
  444.6 79.1 %copy-start.5 = (bf16[1792,512]{1,0:T(8,128)(2,1)S(1)}, bf16[1792,512]{1,0:T(8,128)(2,1)}, u32[]{:S(2)}) copy-start(bf16[1792,512]{1,0:T(8,128)(2,1)} %get-tuple-element.41) | copy-start | bytes 5505028
  444.6 80.3 %copy-start.1 = (bf16[768,512]{1,0:T(8,128)(2,1)S(1)}, bf16[768,512]{1,0:T(8,128)(2,1)}, u32[]{:S(2)}) copy-start(bf16[768,512]{1,0:T(8,128)(2,1)} %param.8) | copy-start | bytes 2359300
  (3 other events, 3.1 us)
Sparse Core Ops, SparseCore 0:
  16.4 84.0 reduce-scatter.17
  104.1 80.7 reduce-scatter.19
  188.5 80.6 reduce-scatter.15
  271.5 57.1 all-gather.4
  332.5 61.8 all-gather.2
  399.7 41.0 all-reduce.2
  443.9 39.6 reduce-scatter.11
  486.6 36.9 reduce-scatter.13
